TPU v7x, 32 devices: a whole 2x2x4 slice. The times are simulated.
32 devices in a mesh: rep: 16 (over z, y, x), shard: 2 (over core).
Axes of the slice: x: 2, y: 2, z: 4, core: 2. Of those that a mesh axis runs over, the one named last changes fastest.
Arguments:
- grad_parts: float32 [16, 2, 2, 1024, 512], P('rep', 'shard'), may hold values from -6 to 6
- weights: bfloat16 [2, 1024, 512], P(None, 'shard'), may hold values from -3 to 3
- stat_left: float32 [2, 1024, 1024], P(None, 'shard'), may hold values from -12 to 332, as said below
- stat_right: float32 [512, 512], replicated, may hold values from -12 to 238.27417, as said below
- basis_left: bfloat16 [2, 1024, 1024], P(None, 'shard'), may hold values from -0.1875 to 0.1875
- basis_right: bfloat16 [512, 512], replicated, may hold values from -0.25 to 0.25
- moment_first: float32 [2, 1024, 512], P(None, 'shard'), may hold values from -2 to 2
- moment_second: float32 [2, 1024, 512], P(None, 'shard'), may hold values from 0.05 to 1
Outputs:
- weights_new: bfloat16 [2, 1024, 512], replicated
- basis_left_new: bfloat16 [2, 1024, 1024], P(None, 'shard')
- basis_right_new: bfloat16 [512, 512], replicated
- moment_first_new: float32 [2, 1024, 512], P(None, 'shard')
- moment_second_new: float32 [2, 1024, 512], P(None, 'shard')
Inputs may be any that keep to these rules, and one draw needn't show every extreme that they name: `stat_left`: each block is a symmetric matrix. `stat_right`: a symmetric matrix.
All inputs are finite; a program needn't handle non-finite values.
Results may differ from a plain program's by a relative error of at most 0.015.
Values may be sent and summed in bfloat16 or wider, within the bound.
A program may use at most 128 MiB of HBM per device.

v0:
```python
import jax
import jax.numpy as jnp
from jax import lax
from jax.sharding import PartitionSpec as P

NS_ITERS = 3
stat_beta = 0.9
moment_decay = 0.9
square_decay = 0.95
learn_rate = 0.1
epsilon = 1e-08
norm_epsilon = 1e-06
schulz_linear = 3.4445
schulz_cubic = -4.775
schulz_quintic = 2.0315


def schulz_whole(matrix):
    current = matrix
    for sweep_index in range(NS_ITERS):
        gram_matrix = lax.optimization_barrier(
            jnp.dot(current, current.T, preferred_element_type=jnp.float32).astype(jnp.bfloat16)
        )
        poly_matrix = (
            schulz_cubic * gram_matrix.astype(jnp.float32)
            + schulz_quintic * jnp.dot(gram_matrix, gram_matrix, preferred_element_type=jnp.float32)
        ).astype(jnp.bfloat16)
        current = (
            schulz_linear * current.astype(jnp.float32)
            + jnp.dot(poly_matrix, current, preferred_element_type=jnp.float32)
        ).astype(jnp.bfloat16)
    return current


def schulz_split(start_rows):
    current = start_rows
    for sweep_index in range(NS_ITERS):
        gathered = lax.all_gather(current, "shard", axis=1, tiled=True)
        gram_rows = lax.optimization_barrier(
            jnp.einsum(
                "bik,bjk->bij", current, gathered, preferred_element_type=jnp.float32
            ).astype(jnp.bfloat16)
        )
        gram_block = lax.all_gather(gram_rows, "shard", axis=1, tiled=True)
        poly_rows = (
            schulz_cubic * gram_rows.astype(jnp.float32)
            + schulz_quintic
            * jnp.einsum("bij,bjk->bik", gram_rows, gram_block, preferred_element_type=jnp.float32)
        ).astype(jnp.bfloat16)
        current = (
            schulz_linear * current.astype(jnp.float32)
            + jnp.einsum("bij,bjk->bik", poly_rows, gathered, preferred_element_type=jnp.float32)
        ).astype(jnp.bfloat16)
    return current


def on_device(
    grad_parts, weights, stat_left, stat_right, basis_left, basis_right, moment_first, moment_second
):
    block_count = weights.shape[0]
    row_count = weights.shape[1]
    width_kv = weights.shape[2]
    rep_count = lax.axis_size("rep")
    shard_pos = lax.axis_index("shard")
    row_start = shard_pos * row_count
    partial_value = grad_parts[0, 0]
    grad_total = lax.psum(partial_value, ("rep", "shard")) / rep_count
    grad_full = grad_total.astype(jnp.bfloat16)
    grad_rows = lax.dynamic_slice_in_dim(grad_full, row_start, row_count, 1)
    left_new = stat_beta * stat_left + (1.0 - stat_beta) * jnp.einsum(
        "bik,bjk->bij", grad_rows, grad_full, preferred_element_type=jnp.float32
    )
    grad_flat = grad_rows.reshape(block_count * row_count, width_kv)
    right_terms = jnp.dot(grad_flat.T, grad_flat, preferred_element_type=jnp.float32)
    right_new = stat_beta * stat_right + (1.0 - stat_beta) * lax.psum(right_terms, "shard")
    basis_all = lax.all_gather(basis_left, "shard", axis=1, tiled=True)
    power_rows = jnp.einsum(
        "bij,bjk->bik", left_new.astype(jnp.bfloat16), basis_all, preferred_element_type=jnp.float32
    )
    local_squares = jnp.sum(power_rows * power_rows, axis=(1, 2))
    block_squares = lax.psum(local_squares, "shard")
    start_rows = (power_rows * lax.rsqrt(block_squares + norm_epsilon)[:, None, None]).astype(
        jnp.bfloat16
    )
    basis_left_new = schulz_split(start_rows)
    right_power = jnp.dot(
        right_new.astype(jnp.bfloat16), basis_right, preferred_element_type=jnp.float32
    )
    right_start = (
        right_power * lax.rsqrt(jnp.sum(right_power * right_power) + norm_epsilon)
    ).astype(jnp.bfloat16)
    basis_right_new = schulz_whole(right_start)
    local_turn = jnp.einsum(
        "bji,bjk->bik", basis_left, grad_rows, preferred_element_type=jnp.float32
    )
    rot_left = lax.psum_scatter(
        local_turn.astype(jnp.bfloat16), "shard", scatter_dimension=1, tiled=True
    ).astype(jnp.float32)
    rot_flat = rot_left.reshape(block_count * row_count, width_kv).astype(jnp.bfloat16)
    rotated = jnp.dot(rot_flat, basis_right, preferred_element_type=jnp.float32).reshape(
        block_count, row_count, width_kv
    )
    moment_new = moment_decay * moment_first + (1.0 - moment_decay) * rotated
    square_new = square_decay * moment_second + (1.0 - square_decay) * rotated * rotated
    direction = moment_new / (jnp.sqrt(square_new) + epsilon)
    direction_flat = direction.reshape(block_count * row_count, width_kv).astype(jnp.bfloat16)
    half_turn = (
        jnp.dot(direction_flat, basis_right.T, preferred_element_type=jnp.float32)
        .astype(jnp.bfloat16)
        .reshape(block_count, row_count, width_kv)
    )
    half_all = lax.all_gather(half_turn, "shard", axis=1, tiled=True)
    update = jnp.einsum("bij,bjk->bik", basis_left, half_all, preferred_element_type=jnp.float32)
    weight_rows_new = (weights.astype(jnp.float32) - learn_rate * update).astype(jnp.bfloat16)
    weights_new = lax.all_gather(weight_rows_new, "shard", axis=1, tiled=True)
    return (weights_new, basis_left_new, basis_right_new, moment_new, square_new)


def solution(mesh):
    placed = (
        P("rep", "shard", None, None, None),
        P(None, "shard", None),
        P(None, "shard", None),
        P(),
        P(None, "shard", None),
        P(),
        P(None, "shard", None),
        P(None, "shard", None),
    )
    return jax.shard_map(
        on_device,
        mesh=mesh,
        in_specs=placed,
        out_specs=(
            P(),
            P(None, "shard", None),
            P(),
            P(None, "shard", None),
            P(None, "shard", None),
        ),
        check_vma=False,
    )
```

profile of v0, /device:TPU:0, one launch (start us, length us, event | category | flops | bytes accessed | tf_op | source)
XLA Modules:
  0.0 368.9 jit_solution(12095255493840172626)
XLA Ops:
  8.0 0.0 copy-start
  8.0 0.0 all-reduce.3.cloned.1.call-start
  8.1 0.7 all-reduce.3.cloned.1.call-update
  8.7 0.0 all-gather.14.cloned.1.call-start
  8.8 0.5 all-gather.14.cloned.1.call-update
  9.3 0.0 all-gather.16.cloned.1.call-start
  9.4 149.6 %all-reduce.3.cloned.1.call-done = f32[2,1024,512]{2,1,0:T(8,128)} async-done(((f32[2,1024,512]{2,1,0:T(8,128)}), f32[2,1024,512]{2,1,0:T(8,128)}) %all-reduce.3.cloned.1.call-update) | async-done | bytes 4194320 | tf_op jit(solution)/shard_map/psum | solution.py:67
  158.9 2.8 multiply_convert_fusion.1
  161.7 0.0 copy-start.2
  161.7 0.0 all-gather.14.cloned.1.call-done
  161.8 9.8 %multiply_reduce_fusion = (f32[2]{0:T(128)S(1)}, f32[2,512,1024]{2,1,0:T(8,128)}) fusion(bf16[2,1024,1024]{2,1,0:T(8,128)(2,1)} %all-gather.14.cloned.1.call-done, f32[2,512,1024]{2,1,0:T(8,128)} %param.10, bf16[2,1024,512]{2,1,0:T(8,128)(2,1)S(1)} %multiply_convert_fusion.1, s32[]{:T(128)S(6)} %select_n.3), kind=kOutput, calls=%fused_computation.7 | convolution fusion | flops 3227516928 | bytes 15728652 | tf_op jit(solution)/shard_map/bij,bjk->bik/dot_general | solution.py:77
  171.6 2.4 psum.22
  174.0 4.1 %multiply_convert_fusion = bf16[2,512,1024]{2,1,0:T(8,128)(2,1)} fusion(f32[2,512,1024]{2,1,0:T(8,128)} %get-tuple-element.14, f32[2]{0:T(128)S(1)} %add_rsqrt_fusion), kind=kLoop, calls=%fused_computation.6 | loop fusion | flops 2097152 | bytes 6291464 | tf_op jit(solution)/shard_map/convert_element_type | solution.py:82
  178.2 0.0 all-gather.16.cloned.1.call-update
  178.2 0.0 copy-start.1
  178.2 0.0 all-gather.18.cloned.1.call-start
  178.3 12.5 %all-gather.16.cloned.1.call-done = bf16[2,1024,1024]{2,1,0:T(8,128)(2,1)} async-done(((bf16[2,512,1024]{2,1,0:T(8,128)(2,1)}), bf16[2,1024,1024]{2,1,0:T(8,128)(2,1)}) %all-gather.16.cloned.1.call-update) | async-done | bytes 4194320 | tf_op jit(solution)/shard_map/all_gather | solution.py:38
  190.8 6.5 %convolution_convert_fusion.2 = bf16[2,512,1024]{2,1,0:T(8,128)(2,1)} fusion(bf16[2,512,1024]{2,1,0:T(8,128)(2,1)} %multiply_convert_fusion, bf16[2,1024,1024]{2,1,0:T(8,128)(2,1)} %all-gather.16.cloned.1.call-done), kind=kOutput, calls=%fused_computation.19 | convolution fusion | flops 2148532224 | bytes 8388608 | tf_op jit(solution)/shard_map/bik,bjk->bij/dot_general | solution.py:40
  197.3 0.0 all-gather.18.cloned.1.call-update
  197.3 0.0 all-gather.20.cloned.1.call-start
  197.4 14.8 %all-gather.18.cloned.1.call-done = bf16[2,1024,1024]{2,1,0:T(8,128)(2,1)} async-done(((bf16[2,512,1024]{2,1,0:T(8,128)(2,1)}), bf16[2,1024,1024]{2,1,0:T(8,128)(2,1)}) %all-gather.18.cloned.1.call-update) | async-done | bytes 4194320 | tf_op jit(solution)/shard_map/all_gather | solution.py:44
  212.2 10.7 %add_convert_fusion.4 = bf16[2,512,1024]{2,1,0:T(8,128)(2,1)} fusion(bf16[2,512,1024]{2,1,0:T(8,128)(2,1)S(1)} %copy-done.1, bf16[2,1024,1024]{2,1,0:T(8,128)(2,1)} %all-gather.16.cloned.1.call-done, bf16[2,512,1024]{2,1,0:T(8,128)(2,1)} %convolution_convert_fusion.2, bf16[2,1024,1024]{2,1,0:T(8,128)(2,1)} %all-gather.18.cloned.1.call-done), kind=kOutput, calls=%fused_computation.4 | convolution fusion | flops 4304404480 | bytes 14680064 | tf_op jit(solution)/shard_map/bij,bjk->bik/dot_general | solution.py:52
  222.9 0.0 all-gather.20.cloned.1.call-update
  222.9 0.0 reduce-scatter.2.cloned.1.call-start
  223.0 4.7 %convert_bitcast_fusion = bf16[2,1024,512]{2,1,0:T(8,128)(2,1)} fusion(bf16[2,512,1024]{2,1,0:T(8,128)(2,1)} %param.12, bf16[2,1024,512]{2,1,0:T(8,128)(2,1)} %copy-done.2, s32[]{:T(128)S(6)} %select_n.3), kind=kOutput, calls=%fused_computation.16 | convolution fusion | flops 1074790400 | bytes 5242884 | tf_op jit(solution)/shard_map/bji,bjk->bik/dot_general | solution.py:93
  227.6 0.0 reduce-scatter.2.cloned.1.call-update
  227.7 0.2 all-gather.22.cloned.1.call-start
  227.9 9.9 %all-gather.20.cloned.1.call-done = bf16[2,1024,1024]{2,1,0:T(8,128)(2,1)} async-done(((bf16[2,512,1024]{2,1,0:T(8,128)(2,1)}), bf16[2,1024,1024]{2,1,0:T(8,128)(2,1)}) %all-gather.20.cloned.1.call-update) | async-done | bytes 4194320 | tf_op jit(solution)/shard_map/all_gather | solution.py:38
  237.8 5.9 %convolution_convert_fusion.1 = bf16[2,512,1024]{2,1,0:T(8,128)(2,1)} fusion(bf16[2,512,1024]{2,1,0:T(8,128)(2,1)S(1)} %copy-done.6, bf16[2,1024,1024]{2,1,0:T(8,128)(2,1)} %all-gather.20.cloned.1.call-done), kind=kOutput, calls=%fused_computation.18 | convolution fusion | flops 2148532224 | bytes 8388608 | tf_op jit(solution)/shard_map/bik,bjk->bij/dot_general | solution.py:40
  243.6 0.0 all-gather.22.cloned.1.call-update
  243.7 0.0 all-gather.10.cloned.1.call-start
  243.7 7.7 %reduce-scatter.2.cloned.1.call-done = bf16[2,512,512]{2,1,0:T(8,128)(2,1)} async-done(((bf16[2,1024,512]{2,1,0:T(8,128)(2,1)}), bf16[2,512,512]{2,1,0:T(8,128)(2,1)}) %reduce-scatter.2.cloned.1.call-update) | async-done | bytes 1048592 | tf_op jit(solution)/shard_map/reduce_scatter | solution.py:96
  251.4 6.2 %divide_convert_fusion = (bf16[2,512,512]{2,1,0:T(8,128)(2,1)S(1)}, f32[2,512,512]{2,1,0:T(8,128)}, f32[2,512,512]{2,1,0:T(8,128)}) fusion(f32[2,512,512]{2,1,0:T(8,128)} %param.15, f32[2,512,512]{2,1,0:T(8,128)} %param.14, bf16[2,512,512]{2,1,0:T(8,128)(2,1)} %reduce-scatter.2.cloned.1.call-done, bf16[512,512]{1,0:T(8,128)(2,1)S(1)} %copy-done), kind=kOutput, calls=%fused_computation.14 | convolution fusion | flops 542113792 | bytes 11010048 | tf_op jit(solution)/shard_map/dot_general | solution.py:100
  257.5 0.7 convolution_convert_fusion.3
  258.3 1.3 copy.14
  259.6 0.0 all-gather.10.cloned.1.call-update
  259.6 0.0 copy-start.3
  259.6 0.0 all-gather.24.cloned.1.call-start
  259.7 8.1 %all-gather.22.cloned.1.call-done = bf16[2,1024,1024]{2,1,0:T(8,128)(2,1)} async-done(((bf16[2,512,1024]{2,1,0:T(8,128)(2,1)}), bf16[2,1024,1024]{2,1,0:T(8,128)(2,1)}) %all-gather.22.cloned.1.call-update) | async-done | bytes 4194320 | tf_op jit(solution)/shard_map/all_gather | solution.py:44
  267.8 11.3 %add_convert_fusion.2 = bf16[2,512,1024]{2,1,0:T(8,128)(2,1)} fusion(bf16[2,512,1024]{2,1,0:T(8,128)(2,1)} %add_convert_fusion.4, bf16[2,1024,1024]{2,1,0:T(8,128)(2,1)} %all-gather.20.cloned.1.call-done, bf16[2,512,1024]{2,1,0:T(8,128)(2,1)} %convolution_convert_fusion.1, bf16[2,1024,1024]{2,1,0:T(8,128)(2,1)} %all-gather.22.cloned.1.call-done), kind=kOutput, calls=%fused_computation.2 | convolution fusion | flops 4304404480 | bytes 14680064 | tf_op jit(solution)/shard_map/bij,bjk->bik/dot_general | solution.py:52
  279.1 0.0 all-gather.24.cloned.1.call-update
  279.1 0.0 all-reduce.5.cloned.1.call-start
  279.2 1.7 convolution_bitcast_fusion
  280.9 0.0 all-reduce.5.cloned.1.call-update
  280.9 0.0 all-gather.12.cloned.1.call-start
  281.0 2.3 copy.13
  283.3 4.9 %fusion.1 = bf16[2,512,512]{1,2,0:T(8,128)(2,1)} fusion(bf16[2,512,512]{1,2,0:T(8,128)(2,1)} %copy.13, bf16[2,1024,512]{1,2,0:T(8,128)(2,1)} %all-gather.10.cloned.1.call-done, bf16[2,512,1024]{2,1,0:T(8,128)(2,1)} %param.12), kind=kOutput, calls=%fused_computation.13 | convolution fusion | flops 1075838976 | bytes 6291456 | tf_op jit(solution)/shard_map/bij,bjk->bik/dot_general | solution.py:113
  288.1 0.0 all-gather.12.cloned.1.call-update
  288.2 0.3 all-gather.26.cloned.1.call-start
  288.4 9.4 %all-gather.24.cloned.1.call-done = bf16[2,1024,1024]{2,1,0:T(8,128)(2,1)} async-done(((bf16[2,512,1024]{2,1,0:T(8,128)(2,1)}), bf16[2,1024,1024]{2,1,0:T(8,128)(2,1)}) %all-gather.24.cloned.1.call-update) | async-done | bytes 4194320 | tf_op jit(solution)/shard_map/all_gather | solution.py:38
  297.8 5.9 %convolution_convert_fusion = bf16[2,512,1024]{2,1,0:T(8,128)(2,1)} fusion(bf16[2,512,1024]{2,1,0:T(8,128)(2,1)S(1)} %copy-done.4, bf16[2,1024,1024]{2,1,0:T(8,128)(2,1)} %all-gather.24.cloned.1.call-done), kind=kOutput, calls=%fused_computation.17 | convolution fusion | flops 2148532224 | bytes 8388608 | tf_op jit(solution)/shard_map/bik,bjk->bij/dot_general | solution.py:40
  303.8 0.0 all-gather.26.cloned.1.call-update
  303.8 16.8 %all-reduce.5.cloned.1.call-done = f32[512,512]{1,0:T(8,128)} async-done(((f32[512,512]{1,0:T(8,128)}), f32[512,512]{1,0:T(8,128)}) %all-reduce.5.cloned.1.call-update) | async-done | bytes 1048592 | tf_op jit(solution)/shard_map/psum | solution.py:75
  320.6 2.7 multiply_reduce_fusion.1
  324.0 0.5 convolution_convert_fusion.6
  324.5 0.7 fusion.8
  325.2 0.5 convolution_convert_fusion.5
  325.7 0.7 fusion.9
  326.4 1.3 convolution_convert_fusion.4
  327.7 3.1 fusion.10
  330.8 3.6 all-gather.12.cloned.1.call-done
  334.4 3.9 %copy.15 = bf16[2,1024,512]{2,1,0:T(8,128)(2,1)} copy(bf16[2,1024,512]{1,2,0:T(8,128)(2,1)} %all-gather.12.cloned.1.call-done) | data formatting | bytes 4194304
  338.4 12.3 %all-gather.26.cloned.1.call-done = bf16[2,1024,1024]{2,1,0:T(8,128)(2,1)} async-done(((bf16[2,512,1024]{2,1,0:T(8,128)(2,1)}), bf16[2,1024,1024]{2,1,0:T(8,128)(2,1)}) %all-gather.26.cloned.1.call-update) | async-done | bytes 4194320 | tf_op jit(solution)/shard_map/all_gather | solution.py:44
  350.6 10.7 %add_convert_fusion = bf16[2,512,1024]{2,1,0:T(8,128)(2,1)} fusion(bf16[2,512,1024]{2,1,0:T(8,128)(2,1)S(1)} %copy-done.5, bf16[2,1024,1024]{2,1,0:T(8,128)(2,1)} %all-gather.24.cloned.1.call-done, bf16[2,512,1024]{2,1,0:T(8,128)(2,1)} %convolution_convert_fusion, bf16[2,1024,1024]{2,1,0:T(8,128)(2,1)} %all-gather.26.cloned.1.call-done), kind=kOutput, calls=%fused_computation | convolution fusion | flops 4304404480 | bytes 14680064 | tf_op jit(solution)/shard_map/bij,bjk->bik/dot_general | solution.py:52
  (12 shorter events, 0.0 us)
Async XLA Ops:
  8.0 243.4 %copy-start = (bf16[512,512]{1,0:T(8,128)(2,1)S(1)}, bf16[512,512]{1,0:T(8,128)(2,1)}, u32[]{:S(2)}) copy-start(bf16[512,512]{1,0:T(8,128)(2,1)} %param.13) | copy-start | bytes 1572868
  8.0 150.9 %all-reduce.3.cloned.1.call-start = ((), (), s32[]{:S(2)}) async-start(), calls=%async_computation.1 | async-start | bytes 8388608 | tf_op jit(solution)/shard_map/psum | solution.py:67
  8.7 153.0 %all-gather.14.cloned.1.call-start = ((), (), s32[]{:S(2)}) async-start(), calls=%async_computation.5 | async-start | bytes 6291456 | tf_op jit(solution)/shard_map/all_gather | solution.py:76
  9.3 181.4 %all-gather.16.cloned.1.call-start = ((), (), s32[]{:S(2)}) async-start(), calls=%async_computation.6 | async-start | bytes 6291456 | tf_op jit(solution)/shard_map/all_gather | solution.py:38
  161.7 9.9 %copy-start.2 = (bf16[2,1024,512]{2,1,0:T(8,128)(2,1)}, bf16[2,1024,512]{2,1,0:T(8,128)(2,1)S(1)}, u32[]{:S(2)}) copy-start(bf16[2,1024,512]{2,1,0:T(8,128)(2,1)S(1)} %multiply_convert_fusion.1) | copy-start | bytes 6291460
  178.2 34.0 %copy-start.1 = (bf16[2,512,1024]{2,1,0:T(8,128)(2,1)S(1)}, bf16[2,512,1024]{2,1,0:T(8,128)(2,1)}, u32[]{:S(2)}) copy-start(bf16[2,512,1024]{2,1,0:T(8,128)(2,1)} %multiply_convert_fusion) | copy-start | bytes 6291460
  178.2 33.9 %all-gather.18.cloned.1.call-start = ((), (), s32[]{:S(2)}) async-start(), calls=%async_computation.7 | async-start | bytes 6291456 | tf_op jit(solution)/shard_map/all_gather | solution.py:44
  197.3 40.5 %all-gather.20.cloned.1.call-start = ((), (), s32[]{:S(2)}) async-start(), calls=%async_computation.8 | async-start | bytes 6291456 | tf_op jit(solution)/shard_map/all_gather | solution.py:38
  222.9 14.9 %copy-start.6 = (bf16[2,512,1024]{2,1,0:T(8,128)(2,1)S(1)}, bf16[2,512,1024]{2,1,0:T(8,128)(2,1)}, u32[]{:S(2)}) copy-start(bf16[2,512,1024]{2,1,0:T(8,128)(2,1)} %add_convert_fusion.4) | copy-start | bytes 6291460
  222.9 28.5 %reduce-scatter.2.cloned.1.call-start = ((), (), s32[]{:S(2)}) async-start(), calls=%async_computation.2 | async-start | bytes 3145728 | tf_op jit(solution)/shard_map/reduce_scatter | solution.py:96
  227.7 40.1 %all-gather.22.cloned.1.call-start = ((), (), s32[]{:S(2)}) async-start(), calls=%async_computation.9 | async-start | bytes 6291456 | tf_op jit(solution)/shard_map/all_gather | solution.py:44
  243.7 39.6 %all-gather.10.cloned.1.call-start = ((), (), s32[]{:S(2)}) async-start(), calls=%async_computation.3 | async-start | bytes 3145728 | tf_op jit(solution)/shard_map/all_gather | solution.py:112
  259.6 19.5 %copy-start.3 = (bf16[2,1024,512]{2,1,0:T(8,128)(2,1)S(1)}, bf16[2,1024,512]{2,1,0:T(8,128)(2,1)}, u32[]{:S(2)}) copy-start(bf16[2,1024,512]{2,1,0:T(8,128)(2,1)} %copy-done.2) | copy-start | bytes 6291460
  259.6 38.2 %all-gather.24.cloned.1.call-start = ((), (), s32[]{:S(2)}) async-start(), calls=%async_computation.10 | async-start | bytes 6291456 | tf_op jit(solution)/shard_map/all_gather | solution.py:38
  279.1 41.5 %all-reduce.5.cloned.1.call-start = ((), (), s32[]{:S(2)}) async-start(), calls=%async_computation.12 | async-start | bytes 2097152 | tf_op jit(solution)/shard_map/psum | solution.py:75
  280.9 53.5 %all-gather.12.cloned.1.call-start = ((), (), s32[]{:S(2)}) async-start(), calls=%async_computation.4 | async-start | bytes 3145728 | tf_op jit(solution)/shard_map/all_gather | solution.py:115
  283.2 14.6 %copy-start.4 = (bf16[2,512,1024]{2,1,0:T(8,128)(2,1)S(1)}, bf16[2,512,1024]{2,1,0:T(8,128)(2,1)}, u32[]{:S(2)}) copy-start(bf16[2,512,1024]{2,1,0:T(8,128)(2,1)} %add_convert_fusion.2) | copy-start | bytes 6291460
  288.2 62.5 %all-gather.26.cloned.1.call-start = ((), (), s32[]{:S(2)}) async-start(), calls=%async_computation.11 | async-start | bytes 6291456 | tf_op jit(solution)/shard_map/all_gather | solution.py:44
  327.7 22.9 %copy-start.5 = (bf16[2,512,1024]{2,1,0:T(8,128)(2,1)S(1)}, bf16[2,512,1024]{2,1,0:T(8,128)(2,1)}, u32[]{:S(2)}) copy-start(bf16[2,512,1024]{2,1,0:T(8,128)(2,1)} %add_convert_fusion.2) | copy-start | bytes 6291460
Sparse Core Ops, SparseCore 0:
  14.4 144.5 all-reduce.2
Sparse Core Ops, SparseCore 1:
  10.8 16.3 all-gather.13
  178.3 12.4 all-gather.15
  197.4 14.7 all-gather.17
  223.0 14.7 all-gather.19
  240.6 10.7 reduce-scatter.1
  253.0 14.7 all-gather.21
  269.8 11.6 all-gather.9
  283.0 14.7 all-gather.23
  300.1 20.4 all-reduce.4
  322.7 11.6 all-gather.11
  335.9 14.7 all-gather.25
where the time goes:
time: 369 us
  waiting for transfers between devices  246 us (67%)
  matrix products  88.6 us (24%)
  between operations  16.6 us (4%)
  local copies, waits for them, and re-layouts  7.58 us (2%)
  other arithmetic  6.91 us (2%)
    psum x1, waiting for transfers between devices, on_device(): grad_total = lax.psum(partial_value, ('rep', 'shard')) / rep_count  150 us
    all_gather x3, waiting for transfers between devices, schulz_split(): gram_block = lax.all_gather(gram_rows, 'shard', axis=1, tiled=True)  35.2 us
    dot_general x3, matrix products, schulz_split(): jnp.einsum('bij,bjk->bik', poly_rows, gathered, preferred_element_type=jn...  32.7 us
    all_gather x3, waiting for transfers between devices, schulz_split(): gathered = lax.all_gather(current, 'shard', axis=1, tiled=True)  31.7 us
    dot_general x3, matrix products, schulz_split(): jnp.einsum('bik,bjk->bij', current, gathered, preferred_element_type=jnp....  18.3 us
    psum x1, waiting for transfers between devices, on_device(): lax.psum(right_terms, 'shard')  16.8 us
    dot_general x1, matrix products, on_device(): jnp.einsum('bij,bjk->bik', left_new.astype(jnp.bfloat16), basis_all, pref...  9.84 us
    reduce_scatter x1, waiting for transfers between devices, on_device(): lax.psum_scatter(local_turn.astype(jnp.bfloat16), 'shard', scatter_dimens...  7.67 us
  transfers between devices with their start and end apart: 12, of which 10 were waited for; matrix products, arithmetic and copies ran while one was open for 17% of the time, Pallas kernels for 0%

commit v1 on v0

--- a/solution.py
+++ b/solution.py
@@ -64,7 +64,7 @@
     shard_pos = lax.axis_index("shard")
     row_start = shard_pos * row_count
     partial_value = grad_parts[0, 0]
-    grad_total = lax.psum(partial_value, ("rep", "shard")) / rep_count
+    grad_total = lax.psum(lax.psum(partial_value, "shard"), "rep") / rep_count
     grad_full = grad_total.astype(jnp.bfloat16)
     grad_rows = lax.dynamic_slice_in_dim(grad_full, row_start, row_count, 1)
     left_new = stat_beta * stat_left + (1.0 - stat_beta) * jnp.einsum(

time: 369 us -> 441 us (1.20)
  waiting for transfers between devices: 246 us -> 321 us
    psum x1 -> x2, waiting for transfers between devices: 150 us -> 209 us  [on_device(): grad_total = lax.psum(lax.psum(partial_value, 'shard'), 'rep') / rep_count]
    all_gather x1, waiting for transfers between devices: 0.03 us -> 11.4 us  [on_device(): basis_all = lax.all_gather(basis_left, 'shard', axis=1, tiled=True)]
  transfers between devices with their start and end apart: 12 -> 13, of which waited for: 10 -> 12; matrix products, arithmetic and copies ran while one was open for 17% -> 14% of each run, Pallas kernels for 0% -> 0%
where the time goes in v1:
time: 441 us
  waiting for transfers between devices  321 us (73%)
  matrix products  87.9 us (20%)
  between operations  14.7 us (3%)
  local copies, waits for them, and re-layouts  7.58 us (2%)
  other arithmetic  6.91 us (2%)
    psum x2, waiting for transfers between devices, on_device(): grad_total = lax.psum(lax.psum(partial_value, 'shard'), 'rep') / rep_count  209 us
    all_gather x3, waiting for transfers between devices, schulz_split(): gram_block = lax.all_gather(gram_rows, 'shard', axis=1, tiled=True)  35.6 us
    all_gather x3, waiting for transfers between devices, schulz_split(): gathered = lax.all_gather(current, 'shard', axis=1, tiled=True)  34.6 us
    dot_general x3, matrix products, schulz_split(): jnp.einsum('bij,bjk->bik', poly_rows, gathered, preferred_element_type=jn...  32.7 us
    dot_general x3, matrix products, schulz_split(): jnp.einsum('bik,bjk->bij', current, gathered, preferred_element_type=jnp....  18.3 us
    psum x1, waiting for transfers between devices, on_device(): lax.psum(right_terms, 'shard')  17.3 us
    all_gather x1, waiting for transfers between devices, on_device(): basis_all = lax.all_gather(basis_left, 'shard', axis=1, tiled=True)  11.4 us
    dot_general x1, matrix products, on_device(): jnp.einsum('bij,bjk->bik', left_new.astype(jnp.bfloat16), basis_all, pref...  9.13 us
  transfers between devices with their start and end apart: 13, of which 12 were waited for; matrix products, arithmetic and copies ran while one was open for 14% of the time, Pallas kernels for 0%

profile of v1, /device:TPU:0, one launch (start us, length us, event | category | flops | bytes accessed | tf_op | source)
XLA Modules:
  0.0 441.0 jit_solution(7393316534938487174)
XLA Ops:
  7.2 0.0 copy-start
  7.2 0.0 all-reduce.4.cloned.1.call-start
  7.2 0.7 all-reduce.4.cloned.1.call-update
  7.9 0.0 all-reduce.6.cloned.1.call-start
  8.0 33.7 %all-reduce.4.cloned.1.call-done = f32[2,1024,512]{2,1,0:T(8,128)} async-done(((f32[2,1024,512]{2,1,0:T(8,128)}), f32[2,1024,512]{2,1,0:T(8,128)}) %all-reduce.4.cloned.1.call-update) | async-done | bytes 4194320 | tf_op jit(solution)/shard_map/psum | solution.py:67
  41.7 0.0 all-reduce.6.cloned.1.call-update
  41.7 0.0 all-gather.14.cloned.1.call-start
  41.8 0.7 all-gather.14.cloned.1.call-update
  42.4 0.0 all-gather.16.cloned.1.call-start
  42.5 175.1 %all-reduce.6.cloned.1.call-done = f32[2,1024,512]{2,1,0:T(8,128)} async-done(((f32[2,1024,512]{2,1,0:T(8,128)}), f32[2,1024,512]{2,1,0:T(8,128)}) %all-reduce.6.cloned.1.call-update) | async-done | bytes 4194320 | tf_op jit(solution)/shard_map/psum | solution.py:67
  217.6 2.8 multiply_convert_fusion.1
  220.4 11.4 %all-gather.14.cloned.1.call-done = bf16[2,1024,1024]{2,1,0:T(8,128)(2,1)} async-done(((bf16[2,512,1024]{2,1,0:T(8,128)(2,1)}), bf16[2,1024,1024]{2,1,0:T(8,128)(2,1)}) %all-gather.14.cloned.1.call-update) | async-done | bytes 4194320 | tf_op jit(solution)/shard_map/all_gather | solution.py:76
  231.8 9.1 %multiply_reduce_fusion = (f32[2]{0:T(128)S(1)}, f32[2,512,1024]{2,1,0:T(8,128)}) fusion(bf16[2,1024,1024]{2,1,0:T(8,128)(2,1)} %all-gather.14.cloned.1.call-done, f32[2,512,1024]{2,1,0:T(8,128)} %param.10, bf16[2,1024,512]{2,1,0:T(8,128)(2,1)S(1)} %multiply_convert_fusion.1, s32[]{:T(128)S(6)} %select_n.3), kind=kOutput, calls=%fused_computation.7 | convolution fusion | flops 3227516928 | bytes 15728652 | tf_op jit(solution)/shard_map/bij,bjk->bik/dot_general | solution.py:77
  241.0 2.4 psum.30
  243.4 4.1 multiply_convert_fusion
  247.6 0.0 all-gather.16.cloned.1.call-update
  247.6 0.0 all-gather.18.cloned.1.call-start
  247.7 14.9 %all-gather.16.cloned.1.call-done = bf16[2,1024,1024]{2,1,0:T(8,128)(2,1)} async-done(((bf16[2,512,1024]{2,1,0:T(8,128)(2,1)}), bf16[2,1024,1024]{2,1,0:T(8,128)(2,1)}) %all-gather.16.cloned.1.call-update) | async-done | bytes 4194320 | tf_op jit(solution)/shard_map/all_gather | solution.py:38
  262.6 6.5 %convolution_convert_fusion.2 = bf16[2,512,1024]{2,1,0:T(8,128)(2,1)} fusion(bf16[2,512,1024]{2,1,0:T(8,128)(2,1)} %multiply_convert_fusion, bf16[2,1024,1024]{2,1,0:T(8,128)(2,1)} %all-gather.16.cloned.1.call-done), kind=kOutput, calls=%fused_computation.19 | convolution fusion | flops 2148532224 | bytes 8388608 | tf_op jit(solution)/shard_map/bik,bjk->bij/dot_general | solution.py:40
  269.1 0.0 all-gather.18.cloned.1.call-update
  269.1 0.0 all-gather.20.cloned.1.call-start
  269.2 14.9 %all-gather.18.cloned.1.call-done = bf16[2,1024,1024]{2,1,0:T(8,128)(2,1)} async-done(((bf16[2,512,1024]{2,1,0:T(8,128)(2,1)}), bf16[2,1024,1024]{2,1,0:T(8,128)(2,1)}) %all-gather.18.cloned.1.call-update) | async-done | bytes 4194320 | tf_op jit(solution)/shard_map/all_gather | solution.py:44
  284.1 10.7 %add_convert_fusion.4 = bf16[2,512,1024]{2,1,0:T(8,128)(2,1)} fusion(bf16[2,512,1024]{2,1,0:T(8,128)(2,1)S(1)} %copy-done.1, bf16[2,1024,1024]{2,1,0:T(8,128)(2,1)} %all-gather.16.cloned.1.call-done, bf16[2,512,1024]{2,1,0:T(8,128)(2,1)} %convolution_convert_fusion.2, bf16[2,1024,1024]{2,1,0:T(8,128)(2,1)} %all-gather.18.cloned.1.call-done), kind=kOutput, calls=%fused_computation.4 | convolution fusion | flops 4304404480 | bytes 14680064 | tf_op jit(solution)/shard_map/bij,bjk->bik/dot_general | solution.py:52
  294.8 0.0 all-gather.20.cloned.1.call-update
  294.9 0.0 reduce-scatter.2.cloned.1.call-start
  294.9 4.7 %convert_bitcast_fusion = bf16[2,1024,512]{2,1,0:T(8,128)(2,1)} fusion(bf16[2,512,1024]{2,1,0:T(8,128)(2,1)} %param.12, bf16[2,1024,512]{2,1,0:T(8,128)(2,1)} %copy-done.2, s32[]{:T(128)S(6)} %select_n.3), kind=kOutput, calls=%fused_computation.16 | convolution fusion | flops 1074790400 | bytes 5242884 | tf_op jit(solution)/shard_map/bji,bjk->bik/dot_general | solution.py:93
  299.6 0.0 reduce-scatter.2.cloned.1.call-update
  299.6 0.2 all-gather.22.cloned.1.call-start
  299.8 10.0 %all-gather.20.cloned.1.call-done = bf16[2,1024,1024]{2,1,0:T(8,128)(2,1)} async-done(((bf16[2,512,1024]{2,1,0:T(8,128)(2,1)}), bf16[2,1024,1024]{2,1,0:T(8,128)(2,1)}) %all-gather.20.cloned.1.call-update) | async-done | bytes 4194320 | tf_op jit(solution)/shard_map/all_gather | solution.py:38
  309.9 5.9 %convolution_convert_fusion.1 = bf16[2,512,1024]{2,1,0:T(8,128)(2,1)} fusion(bf16[2,512,1024]{2,1,0:T(8,128)(2,1)S(1)} %copy-done.6, bf16[2,1024,1024]{2,1,0:T(8,128)(2,1)} %all-gather.20.cloned.1.call-done), kind=kOutput, calls=%fused_computation.18 | convolution fusion | flops 2148532224 | bytes 8388608 | tf_op jit(solution)/shard_map/bik,bjk->bij/dot_general | solution.py:40
  315.7 0.0 all-gather.22.cloned.1.call-update
  315.7 0.0 all-gather.10.cloned.1.call-start
  315.8 7.7 %reduce-scatter.2.cloned.1.call-done = bf16[2,512,512]{2,1,0:T(8,128)(2,1)} async-done(((bf16[2,1024,512]{2,1,0:T(8,128)(2,1)}), bf16[2,512,512]{2,1,0:T(8,128)(2,1)}) %reduce-scatter.2.cloned.1.call-update) | async-done | bytes 1048592 | tf_op jit(solution)/shard_map/reduce_scatter | solution.py:96
  323.5 6.2 %divide_convert_fusion = (bf16[2,512,512]{2,1,0:T(8,128)(2,1)S(1)}, f32[2,512,512]{2,1,0:T(8,128)}, f32[2,512,512]{2,1,0:T(8,128)}) fusion(f32[2,512,512]{2,1,0:T(8,128)} %param.15, f32[2,512,512]{2,1,0:T(8,128)} %param.14, bf16[2,512,512]{2,1,0:T(8,128)(2,1)} %reduce-scatter.2.cloned.1.call-done, bf16[512,512]{1,0:T(8,128)(2,1)S(1)} %copy-done), kind=kOutput, calls=%fused_computation.14 | convolution fusion | flops 542113792 | bytes 11010048 | tf_op jit(solution)/shard_map/dot_general | solution.py:100
  329.6 0.7 convolution_convert_fusion.3
  330.4 1.3 copy.14
  331.7 0.0 all-gather.10.cloned.1.call-update
  331.7 0.0 all-gather.24.cloned.1.call-start
  331.8 8.2 %all-gather.22.cloned.1.call-done = bf16[2,1024,1024]{2,1,0:T(8,128)(2,1)} async-done(((bf16[2,512,1024]{2,1,0:T(8,128)(2,1)}), bf16[2,1024,1024]{2,1,0:T(8,128)(2,1)}) %all-gather.22.cloned.1.call-update) | async-done | bytes 4194320 | tf_op jit(solution)/shard_map/all_gather | solution.py:44
  340.0 11.3 %add_convert_fusion.2 = bf16[2,512,1024]{2,1,0:T(8,128)(2,1)} fusion(bf16[2,512,1024]{2,1,0:T(8,128)(2,1)} %add_convert_fusion.4, bf16[2,1024,1024]{2,1,0:T(8,128)(2,1)} %all-gather.20.cloned.1.call-done, bf16[2,512,1024]{2,1,0:T(8,128)(2,1)} %convolution_convert_fusion.1, bf16[2,1024,1024]{2,1,0:T(8,128)(2,1)} %all-gather.22.cloned.1.call-done), kind=kOutput, calls=%fused_computation.2 | convolution fusion | flops 4304404480 | bytes 14680064 | tf_op jit(solution)/shard_map/bij,bjk->bik/dot_general | solution.py:52
  351.3 0.0 all-gather.24.cloned.1.call-update
  351.3 0.0 all-reduce.8.cloned.1.call-start
  351.4 1.7 convolution_bitcast_fusion
  353.1 0.0 all-reduce.8.cloned.1.call-update
  353.1 0.0 all-gather.12.cloned.1.call-start
  353.2 2.3 copy.13
  355.5 4.9 %fusion.1 = bf16[2,512,512]{1,2,0:T(8,128)(2,1)} fusion(bf16[2,512,512]{1,2,0:T(8,128)(2,1)} %copy.13, bf16[2,1024,512]{1,2,0:T(8,128)(2,1)} %all-gather.10.cloned.1.call-done, bf16[2,512,1024]{2,1,0:T(8,128)(2,1)} %param.12), kind=kOutput, calls=%fused_computation.13 | convolution fusion | flops 1075838976 | bytes 6291456 | tf_op jit(solution)/shard_map/bij,bjk->bik/dot_general | solution.py:113
  360.3 0.0 all-gather.12.cloned.1.call-update
  360.4 0.3 all-gather.26.cloned.1.call-start
  360.6 9.7 %all-gather.24.cloned.1.call-done = bf16[2,1024,1024]{2,1,0:T(8,128)(2,1)} async-done(((bf16[2,512,1024]{2,1,0:T(8,128)(2,1)}), bf16[2,1024,1024]{2,1,0:T(8,128)(2,1)}) %all-gather.24.cloned.1.call-update) | async-done | bytes 4194320 | tf_op jit(solution)/shard_map/all_gather | solution.py:38
  370.3 5.9 %convolution_convert_fusion = bf16[2,512,1024]{2,1,0:T(8,128)(2,1)} fusion(bf16[2,512,1024]{2,1,0:T(8,128)(2,1)S(1)} %copy-done.4, bf16[2,1024,1024]{2,1,0:T(8,128)(2,1)} %all-gather.24.cloned.1.call-done), kind=kOutput, calls=%fused_computation.17 | convolution fusion | flops 2148532224 | bytes 8388608 | tf_op jit(solution)/shard_map/bik,bjk->bij/dot_general | solution.py:40
  376.2 0.0 all-gather.26.cloned.1.call-update
  376.3 17.3 %all-reduce.8.cloned.1.call-done = f32[512,512]{1,0:T(8,128)} async-done(((f32[512,512]{1,0:T(8,128)}), f32[512,512]{1,0:T(8,128)}) %all-reduce.8.cloned.1.call-update) | async-done | bytes 1048592 | tf_op jit(solution)/shard_map/psum | solution.py:75
  393.6 2.7 multiply_reduce_fusion.1
  397.0 0.5 convolution_convert_fusion.6
  397.5 0.7 fusion.8
  398.2 0.5 convolution_convert_fusion.5
  398.7 0.7 fusion.9
  399.4 1.3 convolution_convert_fusion.4
  400.7 3.1 fusion.10
  403.8 3.5 all-gather.12.cloned.1.call-done
  407.3 3.9 copy.15
  411.3 12.5 %all-gather.26.cloned.1.call-done = bf16[2,1024,1024]{2,1,0:T(8,128)(2,1)} async-done(((bf16[2,512,1024]{2,1,0:T(8,128)(2,1)}), bf16[2,1024,1024]{2,1,0:T(8,128)(2,1)}) %all-gather.26.cloned.1.call-update) | async-done | bytes 4194320 | tf_op jit(solution)/shard_map/all_gather | solution.py:44
  423.8 10.7 %add_convert_fusion = bf16[2,512,1024]{2,1,0:T(8,128)(2,1)} fusion(bf16[2,512,1024]{2,1,0:T(8,128)(2,1)S(1)} %copy-done.5, bf16[2,1024,1024]{2,1,0:T(8,128)(2,1)} %all-gather.24.cloned.1.call-done, bf16[2,512,1024]{2,1,0:T(8,128)(2,1)} %convolution_convert_fusion, bf16[2,1024,1024]{2,1,0:T(8,128)(2,1)} %all-gather.26.cloned.1.call-done), kind=kOutput, calls=%fused_computation | convolution fusion | flops 4304404480 | bytes 14680064 | tf_op jit(solution)/shard_map/bij,bjk->bik/dot_general | solution.py:52
  (15 shorter events, 0.0 us)
Async XLA Ops:
  7.2 316.3 %copy-start = (bf16[512,512]{1,0:T(8,128)(2,1)S(1)}, bf16[512,512]{1,0:T(8,128)(2,1)}, u32[]{:S(2)}) copy-start(bf16[512,512]{1,0:T(8,128)(2,1)} %param.13) | copy-start | bytes 1572868
  7.2 34.5 %all-reduce.4.cloned.1.call-start = ((), (), s32[]{:S(2)}) async-start(), calls=%async_computation.1 | async-start | bytes 8388608 | tf_op jit(solution)/shard_map/psum | solution.py:67
  7.9 209.7 %all-reduce.6.cloned.1.call-start = ((), (), s32[]{:S(2)}) async-start(), calls=%async_computation.2 | async-start | bytes 8388608 | tf_op jit(solution)/shard_map/psum | solution.py:67
  41.7 190.1 %all-gather.14.cloned.1.call-start = ((), (), s32[]{:S(2)}) async-start(), calls=%async_computation.6 | async-start | bytes 6291456 | tf_op jit(solution)/shard_map/all_gather | solution.py:76
  42.4 220.2 %all-gather.16.cloned.1.call-start = ((), (), s32[]{:S(2)}) async-start(), calls=%async_computation.7 | async-start | bytes 6291456 | tf_op jit(solution)/shard_map/all_gather | solution.py:38
  220.4 20.6 %copy-start.2 = (bf16[2,1024,512]{2,1,0:T(8,128)(2,1)}, bf16[2,1024,512]{2,1,0:T(8,128)(2,1)S(1)}, u32[]{:S(2)}) copy-start(bf16[2,1024,512]{2,1,0:T(8,128)(2,1)S(1)} %multiply_convert_fusion.1) | copy-start | bytes 6291460
  247.6 36.5 %copy-start.1 = (bf16[2,512,1024]{2,1,0:T(8,128)(2,1)S(1)}, bf16[2,512,1024]{2,1,0:T(8,128)(2,1)}, u32[]{:S(2)}) copy-start(bf16[2,512,1024]{2,1,0:T(8,128)(2,1)} %multiply_convert_fusion) | copy-start | bytes 6291460
  247.6 36.5 %all-gather.18.cloned.1.call-start = ((), (), s32[]{:S(2)}) async-start(), calls=%async_computation.8 | async-start | bytes 6291456 | tf_op jit(solution)/shard_map/all_gather | solution.py:44
  269.1 40.7 %all-gather.20.cloned.1.call-start = ((), (), s32[]{:S(2)}) async-start(), calls=%async_computation.9 | async-start | bytes 6291456 | tf_op jit(solution)/shard_map/all_gather | solution.py:38
  294.8 15.0 %copy-start.6 = (bf16[2,512,1024]{2,1,0:T(8,128)(2,1)S(1)}, bf16[2,512,1024]{2,1,0:T(8,128)(2,1)}, u32[]{:S(2)}) copy-start(bf16[2,512,1024]{2,1,0:T(8,128)(2,1)} %add_convert_fusion.4) | copy-start | bytes 6291460
  294.9 28.6 %reduce-scatter.2.cloned.1.call-start = ((), (), s32[]{:S(2)}) async-start(), calls=%async_computation.3 | async-start | bytes 3145728 | tf_op jit(solution)/shard_map/reduce_scatter | solution.py:96
  299.6 40.4 %all-gather.22.cloned.1.call-start = ((), (), s32[]{:S(2)}) async-start(), calls=%async_computation.10 | async-start | bytes 6291456 | tf_op jit(solution)/shard_map/all_gather | solution.py:44
  315.7 39.7 %all-gather.10.cloned.1.call-start = ((), (), s32[]{:S(2)}) async-start(), calls=%async_computation.4 | async-start | bytes 3145728 | tf_op jit(solution)/shard_map/all_gather | solution.py:112
  331.7 19.6 %copy-start.3 = (bf16[2,1024,512]{2,1,0:T(8,128)(2,1)S(1)}, bf16[2,1024,512]{2,1,0:T(8,128)(2,1)}, u32[]{:S(2)}) copy-start(bf16[2,1024,512]{2,1,0:T(8,128)(2,1)} %copy-done.2) | copy-start | bytes 6291460
  331.7 38.6 %all-gather.24.cloned.1.call-start = ((), (), s32[]{:S(2)}) async-start(), calls=%async_computation.11 | async-start | bytes 6291456 | tf_op jit(solution)/shard_map/all_gather | solution.py:38
  351.3 42.3 %all-reduce.8.cloned.1.call-start = ((), (), s32[]{:S(2)}) async-start(), calls=%async_computation.13 | async-start | bytes 2097152 | tf_op jit(solution)/shard_map/psum | solution.py:75
  353.1 54.2 %all-gather.12.cloned.1.call-start = ((), (), s32[]{:S(2)}) async-start(), calls=%async_computation.5 | async-start | bytes 3145728 | tf_op jit(solution)/shard_map/all_gather | solution.py:115
  355.4 14.9 %copy-start.4 = (bf16[2,512,1024]{2,1,0:T(8,128)(2,1)S(1)}, bf16[2,512,1024]{2,1,0:T(8,128)(2,1)}, u32[]{:S(2)}) copy-start(bf16[2,512,1024]{2,1,0:T(8,128)(2,1)} %add_convert_fusion.2) | copy-start | bytes 6291460
  360.4 63.4 %all-gather.26.cloned.1.call-start = ((), (), s32[]{:S(2)}) async-start(), calls=%async_computation.12 | async-start | bytes 6291456 | tf_op jit(solution)/shard_map/all_gather | solution.py:44
  400.7 23.1 %copy-start.5 = (bf16[2,512,1024]{2,1,0:T(8,128)(2,1)S(1)}, bf16[2,512,1024]{2,1,0:T(8,128)(2,1)}, u32[]{:S(2)}) copy-start(bf16[2,512,1024]{2,1,0:T(8,128)(2,1)} %add_convert_fusion.2) | copy-start | bytes 6291460
Sparse Core Ops, SparseCore 0:
  10.5 31.1 all-reduce.3
  48.2 169.3 all-reduce.5
  219.2 12.6 all-gather.13
  247.7 14.8 all-gather.15
  269.2 14.8 all-gather.17
  295.0 14.8 all-gather.19
  312.7 10.7 reduce-scatter.1
  325.1 14.8 all-gather.21
  342.2 11.7 all-gather.9
  355.4 14.8 all-gather.23
  372.8 20.7 all-reduce.7
  395.5 11.7 all-gather.11
  408.9 14.8 all-gather.25
